TPU v7x, 512 devices: a whole 4x8x8 slice. The times are simulated.
512 devices in a mesh: section: 16 (over x_lo, z), dp: 32 (over x_hi, y, core).
Axes of the slice: x: 4 (x_hi: 2, x_lo: 2; x = x_hi * 2 + x_lo), y: 8, z: 8, core: 2. Of those that a mesh axis runs over, the one named last changes fastest.
Arguments:
- acts_down: bfloat16 [3, 16, 32, 16, 16, 256], P(None, 'section', 'dp'), may hold values from -6 to 6
- acts_up: bfloat16 [3, 16, 32, 16, 16, 256], P(None, 'section', 'dp'), may hold values from -6 to 6
- front_down: bfloat16 [16, 32, 16, 16, 256], P('section', 'dp'), may hold values from -6 to 6
- front_up: bfloat16 [16, 32, 16, 16, 256], P('section', 'dp'), may hold values from -6 to 6
- master: float32 [16, 2304, 256], P('section', 'dp'), may hold values from -4 to 4
- moment_first: float32 [16, 2304, 256], P('section', 'dp'), may hold values from -36 to 36
- moment_second: float32 [16, 2304, 256], P('section', 'dp'), may hold values from 10 to 100
Outputs:
- dx_down: bfloat16 [3, 16, 32, 16, 16, 256], P(None, 'section', 'dp')
- dx_up: bfloat16 [3, 16, 32, 16, 16, 256], P(None, 'section', 'dp')
- new_weight: bfloat16 [16, 2304, 256], P('section', 'dp')
- new_master: float32 [16, 2304, 256], P('section', 'dp')
- new_first: float32 [16, 2304, 256], P('section', 'dp')
- new_second: float32 [16, 2304, 256], P('section', 'dp')
All inputs are finite; a program needn't handle non-finite values.
Results may differ from a plain program's by a relative error of at most 0.0025.
The roundings to bfloat16 on the way count: a program that leaves them out, or rounds other values in their place, can miss the bound.
Values may be sent and summed in bfloat16 or wider, within the bound.
No kernel may reach another device: no remote copies, remote signals or barrier semaphores. Data moves between devices by JAX's collectives and lax.ppermute only.
A program may use at most 64 MiB of HBM per device.

v0:
```python
import jax
import jax.numpy as jnp
from jax import lax
from jax.sharding import PartitionSpec as P

TICKS = 3
beta_first = 0.9
beta_second = 0.95
learn_rate = 0.01
decay_rate = 0.1
epsilon = 1e-08


def from_partner(value, axis, stride):
    return lax.ppermute(value, axis, [(i, i ^ 1 << stride) for i in range(lax.axis_size(axis))])


def passed_along(value, axis, by):
    length = lax.axis_size(axis)
    pairs = [(i, i + by) for i in range(length) if 0 <= i + by < length]
    return lax.ppermute(value, axis, pairs)


def shifted_taps(feature, direction):
    images, height, columns, channels = feature.shape
    padded = jnp.pad(feature, ((0, 0), (1, 1), (1, 1), (0, 0)))
    pieces = []
    for row_step in range(3):
        for col_step in range(3):
            row_start = 1 + direction * (row_step - 1)
            col_start = 1 + direction * (col_step - 1)
            pieces.append(
                padded[:, row_start : row_start + height, col_start : col_start + columns, :]
            )
    return jnp.concatenate(pieces, axis=3).reshape(images * height * columns, 9 * channels)


def section_front(inputs, incoming, weight):
    channels = inputs.shape[-1]
    factor = (9 * channels) ** (-0.5)
    taps_front = shifted_taps(incoming, -1).reshape(-1, 9, channels)
    kernel = weight.reshape(9, channels, channels)
    grad_hidden = lax.dot_general(
        taps_front, kernel, (((1, 2), (0, 2)), ((), ())), preferred_element_type=jnp.float32
    )
    grad_hidden = factor * grad_hidden.reshape(inputs.shape)
    widened = inputs.astype(jnp.float32)
    hidden, pullback = jax.vjp(jax.nn.gelu, widened)
    outgoing = (incoming.astype(jnp.float32) + pullback(grad_hidden)[0]).astype(jnp.bfloat16)
    return (outgoing, hidden.astype(jnp.bfloat16))


def weight_term(hiddens, seen):
    channels = hiddens[0].shape[-1]
    factor = (9 * channels) ** (-0.5)
    summed = jnp.zeros((9 * channels, channels), jnp.float32)
    for hidden, incoming in zip(hiddens, seen):
        taps_hidden = shifted_taps(hidden, 1)
        summed = summed + lax.dot_general(
            taps_hidden,
            incoming.reshape(-1, channels),
            (((0,), (0,)), ((), ())),
            preferred_element_type=jnp.float32,
        )
    return factor * summed


def per_device(acts_down, acts_up, front_down, front_up, master, moment_first, moment_second):
    sections = lax.axis_size("section")
    own_rows = master[0].astype(jnp.bfloat16)
    mirror_rows = own_rows
    for bit_number in range(sections.bit_length() - 1):
        mirror_rows = from_partner(mirror_rows, "section", bit_number)
    own_weight, mirror_weight = (
        lax.all_gather(own_rows, "dp", axis=0, tiled=True),
        lax.all_gather(mirror_rows, "dp", axis=0, tiled=True),
    )
    grad_down = front_down[0]
    grad_up = front_up[0]
    seen_down = []
    seen_up = []
    hidden_down = []
    hidden_up = []
    outs_down = []
    outs_up = []
    for tick_index in range(TICKS):
        seen_down.append(grad_down)
        seen_up.append(grad_up)
        next_down, hid_down = section_front(acts_down[tick_index, 0], grad_down, own_weight)
        next_up, hid_up = section_front(acts_up[tick_index, 0], grad_up, mirror_weight)
        hidden_down.append(hid_down)
        hidden_up.append(hid_up)
        outs_down.append(next_down)
        outs_up.append(next_up)
        if tick_index + 1 < TICKS:
            grad_down = passed_along(next_down, "section", -1)
            grad_up = passed_along(next_up, "section", 1)
    term_down = weight_term(hidden_down, seen_down)
    term_up = weight_term(hidden_up, seen_up)
    full_down, full_up = (
        lax.psum(term_down.astype(jnp.bfloat16), "dp").astype(jnp.float32),
        lax.psum(term_up.astype(jnp.bfloat16), "dp").astype(jnp.float32),
    )
    shard_rows = term_down.shape[0] // lax.axis_size("dp")
    row_start = lax.axis_index("dp") * shard_rows
    down_rows = lax.dynamic_slice_in_dim(full_down, row_start, shard_rows, 0)
    up_rows = lax.dynamic_slice_in_dim(full_up, row_start, shard_rows, 0)
    mirror_grad = up_rows
    for bit_number in range(sections.bit_length() - 1):
        mirror_grad = from_partner(mirror_grad.astype(jnp.bfloat16), "section", bit_number).astype(
            mirror_grad.dtype
        )
    gradient = down_rows + mirror_grad
    old_master = master[0]
    new_first = beta_first * moment_first[0] + (1.0 - beta_first) * gradient
    new_second = beta_second * moment_second[0] + (1.0 - beta_second) * gradient * gradient
    new_master = old_master - learn_rate * (
        new_first / (jnp.sqrt(new_second) + epsilon) + decay_rate * old_master
    )
    return (
        jnp.stack(outs_down)[:, None],
        jnp.stack(outs_up)[:, None],
        new_master.astype(jnp.bfloat16)[None],
        new_master[None],
        new_first[None],
        new_second[None],
    )


def solution(mesh):
    placed = (
        P(None, "section", "dp", None, None, None),
        P(None, "section", "dp", None, None, None),
        P("section", "dp", None, None, None),
        P("section", "dp", None, None, None),
        P("section", "dp", None),
        P("section", "dp", None),
        P("section", "dp", None),
    )
    return jax.shard_map(
        per_device,
        mesh=mesh,
        in_specs=placed,
        out_specs=(
            P(None, "section", "dp", None, None, None),
            P(None, "section", "dp", None, None, None),
            P("section", "dp", None),
            P("section", "dp", None),
            P("section", "dp", None),
            P("section", "dp", None),
        ),
        check_vma=False,
    )
```

profile of v0, /device:TPU:2, one launch (start us, length us, event | category | flops | bytes accessed | tf_op | source)
XLA Modules:
  0.0 534.1 jit_solution(15789119350843120180)
XLA Ops:
  7.2 1.5 bitcast_convert_fusion
  8.8 4.3 collective-permute-start.2
  13.1 1.0 constant_dynamic-update-slice_fusion.8
  14.1 0.9 constant_dynamic-update-slice_fusion.7
  15.0 0.9 constant_dynamic-update-slice_fusion.6
  16.0 0.9 constant_dynamic-update-slice_fusion.5
  17.1 1.0 copy-done.5
  20.6 1.0 copy-done.15
  26.0 0.9 constant_dynamic-update-slice_fusion.67
  27.7 0.8 pad_slice_fusion.40
  32.8 6.1 %collective-permute-start.3 = (bf16[72,256]{1,0:T(8,128)(2,1)S(1)}, bf16[72,256]{1,0:T(8,128)(2,1)S(1)}, u32[]{:S(2)}, u32[]{:S(2)}) collective-permute-start(bf16[72,256]{1,0:T(8,128)(2,1)S(1)} %collective-permute-done.2), channel_id=1, source_target_pairs={{0,64},{32,96},{64,0},{96,32},{128,192},{160,224},{192,128},{224,1... | collective-permute-start | bytes 110600 | tf_op jit(solution)/shard_map/ppermute | solution.py:15
  39.5 1.2 collective-permute-done.3
  40.8 9.1 %collective-permute-start.4 = (bf16[72,256]{1,0:T(8,128)(2,1)S(1)}, bf16[72,256]{1,0:T(8,128)(2,1)S(1)}, u32[]{:S(2)}, u32[]{:S(2)}) collective-permute-start(bf16[72,256]{1,0:T(8,128)(2,1)S(1)} %collective-permute-done.3), channel_id=1, source_target_pairs={{0,128},{32,160},{64,192},{96,224},{128,0},{160,32},{192,64},{224,... | collective-permute-start | bytes 110600 | tf_op jit(solution)/shard_map/ppermute | solution.py:15
  50.6 1.3 collective-permute-done.4
  51.9 2.8 collective-permute-start.5
  55.4 3.5 dot_general.48
  60.3 3.3 fusion.219
  63.5 35.4 %all-gather.3.cloned.1.call-done = bf16[2304,256]{1,0:T(8,128)(2,1)} async-done(((bf16[72,256]{1,0:T(8,128)(2,1)}), bf16[2304,256]{1,0:T(8,128)(2,1)}) %all-gather.3.cloned.1.call-update) | async-done | bytes 1179664 | tf_op jit(solution)/shard_map/all_gather | solution.py:75
  98.9 2.9 fusion.119
  101.8 6.8 %collective-permute-start = (bf16[1,16,16,256]{3,2,1,0:T(8,128)(2,1)S(1)}, bf16[1,16,16,256]{3,2,1,0:T(8,128)(2,1)S(1)}, u32[]{:S(2)}, u32[]{:S(2)}) collective-permute-start(bf16[1,16,16,256]{3,2,1,0:T(8,128)(2,1)S(1)} %bitcast.548), channel_id=1, source_target_pairs={{32,0},{64,32},{96,64},{128,96},{160,128},{192,160},{224,192},{256... | collective-permute-start | bytes 393224 | tf_op jit(solution)/shard_map/ppermute | solution.py:21
  109.2 3.6 dot_general.54
  119.9 3.5 dot_general.50
  123.4 3.5 fusion.125
  126.9 4.6 collective-permute-start.1
  131.6 51.5 %all-gather.5.cloned.1.call-done = bf16[2304,256]{1,0:T(8,128)(2,1)} async-done(((bf16[72,256]{1,0:T(8,128)(2,1)}), bf16[2304,256]{1,0:T(8,128)(2,1)}) %all-gather.5.cloned.1.call-update) | async-done | bytes 1179664 | tf_op jit(solution)/shard_map/all_gather | solution.py:76
  183.1 3.0 fusion.139
  186.1 3.7 collective-permute-start.6
  189.8 2.0 convolution_bitcast_fusion.2
  191.8 4.9 collective-permute-done.6
  203.0 3.5 dot_general.56
  206.5 3.0 fusion.145
  209.6 2.1 collective-permute-start.7
  211.7 3.7 fusion.7
  215.3 3.4 collective-permute-done.7
  219.3 1.7 fusion.6
  227.4 2.4 dot_general.52
  229.8 2.2 fusion.211
  232.0 1.7 maximum_bitcast_fusion
  238.7 256.8 %all-reduce.15.cloned.1.call-done = (bf16[2304,256]{1,0:T(8,128)(2,1)}, bf16[2304,256]{1,0:T(8,128)(2,1)}) async-done(((bf16[2304,256]{1,0:T(8,128)(2,1)}, bf16[2304,256]{1,0:T(8,128)(2,1)}), (bf16[2304,256]{1,0:T(8,128)(2,1)}, bf16[2304,256]{1,0:T(8,128)(2,1)})) %all-reduce.15.cloned.1.call-update) | async-done | bytes 2359312 | tf_op jit(solution)/shard_map/psum | solution.py:102
  496.2 3.5 collective-permute-start.8
  500.4 1.6 collective-permute-done.8
  502.0 4.6 collective-permute-start.9
  507.4 2.4 dot_general.58
  509.9 7.3 %collective-permute-start.10 = (bf16[72,256]{1,0:T(8,128)(2,1)S(1)}, bf16[72,256]{1,0:T(8,128)(2,1)S(1)}, u32[]{:S(2)}, u32[]{:S(2)}) collective-permute-start(bf16[72,256]{1,0:T(8,128)(2,1)S(1)} %collective-permute-done.9), channel_id=1, source_target_pairs={{0,128},{32,160},{64,192},{96,224},{128,0},{160,32},{192,64},{224,... | collective-permute-start | bytes 110600 | tf_op jit(solution)/shard_map/ppermute | solution.py:15
  517.2 2.2 fusion.194
  520.2 2.2 collective-permute-start.11
  523.2 2.8 collective-permute-done.11
  526.0 1.5 convert_bitcast_fusion.8
  (154 shorter events, 44.8 us)
Async XLA Ops:
  7.2 9.8 %copy-start = (bf16[1,1,16,16,256]{4,3,2,1,0:T(8,128)(2,1)S(1)}, bf16[1,1,16,16,256]{4,3,2,1,0:T(8,128)(2,1)}, u32[]{:S(2)}) copy-start(bf16[1,1,16,16,256]{4,3,2,1,0:T(8,128)(2,1)} %param.9) | copy-start | bytes 393220
  7.2 91.8 %all-gather.3.cloned.1.call-start = ((), (), s32[]{:S(2)}) async-start(), calls=%async_computation | async-start | bytes 1216512 | tf_op jit(solution)/shard_map/all_gather | solution.py:75
  8.8 174.3 %all-gather.5.cloned.1.call-start = ((), (), s32[]{:S(2)}) async-start(), calls=%async_computation.1 | async-start | bytes 1216512 | tf_op jit(solution)/shard_map/all_gather | solution.py:76
  8.8 23.9 %collective-permute-start.2 = (bf16[72,256]{1,0:T(8,128)(2,1)}, bf16[72,256]{1,0:T(8,128)(2,1)S(1)}, u32[]{:S(2)}, u32[]{:S(2)}) collective-permute-start(bf16[72,256]{1,0:T(8,128)(2,1)} %bitcast_convert_fusion), channel_id=1, source_target_pairs={{0,32},{32,0},{64,96},{96,64},{128,160},{160,128},{192,224},{224,1... | collective-permute-start | bytes 110600 | tf_op jit(solution)/shard_map/ppermute | solution.py:15
  13.1 5.0 copy-start.1
  17.1 1.0 copy-start.5
  18.1 1.0 copy-start.4
  19.1 1.0 copy-start.6
  20.6 1.0 copy-start.15
  21.6 1.0 copy-start.3
  22.6 3.3 copy-start.13
  32.7 17.9 %copy-start.17 = (bf16[1,16,16,2304]{3,2,1,0:T(8,128)(2,1)}, bf16[1,16,16,2304]{3,2,1,0:T(8,128)(2,1)S(1)}, u32[]{:S(2)}) copy-start(bf16[1,16,16,2304]{3,2,1,0:T(8,128)(2,1)S(1)} %constant_dynamic-update-slice_fusion.72) | copy-start | bytes 3538948
  32.8 8.0 %collective-permute-start.3 = (bf16[72,256]{1,0:T(8,128)(2,1)S(1)}, bf16[72,256]{1,0:T(8,128)(2,1)S(1)}, u32[]{:S(2)}, u32[]{:S(2)}) collective-permute-start(bf16[72,256]{1,0:T(8,128)(2,1)S(1)} %collective-permute-done.2), channel_id=1, source_target_pairs={{0,64},{32,96},{64,0},{96,32},{128,192},{160,224},{192,128},{224,1... | collective-permute-start | bytes 110600 | tf_op jit(solution)/shard_map/ppermute | solution.py:15
  40.8 11.1 %collective-permute-start.4 = (bf16[72,256]{1,0:T(8,128)(2,1)S(1)}, bf16[72,256]{1,0:T(8,128)(2,1)S(1)}, u32[]{:S(2)}, u32[]{:S(2)}) collective-permute-start(bf16[72,256]{1,0:T(8,128)(2,1)S(1)} %collective-permute-done.3), channel_id=1, source_target_pairs={{0,128},{32,160},{64,192},{96,224},{128,0},{160,32},{192,64},{224,... | collective-permute-start | bytes 110600 | tf_op jit(solution)/shard_map/ppermute | solution.py:15
  51.9 7.0 %collective-permute-start.5 = (bf16[72,256]{1,0:T(8,128)(2,1)S(1)}, bf16[72,256]{1,0:T(8,128)(2,1)S(1)}, u32[]{:S(2)}, u32[]{:S(2)}) collective-permute-start(bf16[72,256]{1,0:T(8,128)(2,1)S(1)} %collective-permute-done.4), channel_id=1, source_target_pairs={{0,256},{32,288},{64,320},{96,352},{128,384},{160,416},{192,448},{... | collective-permute-start | bytes 110600 | tf_op jit(solution)/shard_map/ppermute | solution.py:15
  58.9 0.6 copy-start.12
  59.5 435.9 %all-reduce.15.cloned.1.call-start = ((), (), s32[]{:S(2)}) async-start(), calls=%async_computation.2 | async-start | bytes 4718592 | tf_op jit(solution)/shard_map/psum | solution.py:102
  101.8 11.7 %collective-permute-start = (bf16[1,16,16,256]{3,2,1,0:T(8,128)(2,1)S(1)}, bf16[1,16,16,256]{3,2,1,0:T(8,128)(2,1)S(1)}, u32[]{:S(2)}, u32[]{:S(2)}) collective-permute-start(bf16[1,16,16,256]{3,2,1,0:T(8,128)(2,1)S(1)} %bitcast.548), channel_id=1, source_target_pairs={{32,0},{64,32},{96,64},{128,96},{160,128},{192,160},{224,192},{256... | collective-permute-start | bytes 393224 | tf_op jit(solution)/shard_map/ppermute | solution.py:21
  126.9 62.9 %collective-permute-start.1 = (bf16[1,16,16,256]{3,2,1,0:T(8,128)(2,1)}, bf16[1,16,16,256]{3,2,1,0:T(8,128)(2,1)S(1)}, u32[]{:S(2)}, u32[]{:S(2)}) collective-permute-start(bf16[1,16,16,256]{3,2,1,0:T(8,128)(2,1)} %fusion.125), channel_id=1, source_target_pairs={{32,0},{64,32},{96,64},{128,96},{160,128},{192,160},{224,192},{256... | collective-permute-start | bytes 393224 | tf_op jit(solution)/shard_map/ppermute | solution.py:21
  183.1 6.8 %copy-start.18 = (bf16[1,16,16,2304]{3,2,1,0:T(8,128)(2,1)S(1)}, bf16[1,16,16,2304]{3,2,1,0:T(8,128)(2,1)}, u32[]{:S(2)}) copy-start(bf16[1,16,16,2304]{3,2,1,0:T(8,128)(2,1)} %copy-done.17) | copy-start | bytes 3538948
  186.1 10.6 %collective-permute-start.6 = (bf16[1,16,16,256]{3,2,1,0:T(8,128)(2,1)S(1)}, bf16[1,16,16,256]{3,2,1,0:T(8,128)(2,1)S(1)}, u32[]{:S(2)}, u32[]{:S(2)}) collective-permute-start(bf16[1,16,16,256]{3,2,1,0:T(8,128)(2,1)S(1)} %bitcast.546), channel_id=1, source_target_pairs={{0,32},{32,64},{64,96},{96,128},{128,160},{160,192},{192,224},{224... | collective-permute-start | bytes 393224 | tf_op jit(solution)/shard_map/ppermute | solution.py:21
  206.5 5.1 copy-start.2
  209.6 5.8 %copy-start.8 = (bf16[1,16,16,256]{3,2,1,0:T(8,128)(2,1)}, bf16[1,16,16,256]{3,2,1,0:T(8,128)(2,1)S(1)}, u32[]{:S(2)}) copy-start(bf16[1,16,16,256]{3,2,1,0:T(8,128)(2,1)S(1)} %fusion.145) | copy-start | bytes 393220
  209.6 9.2 %copy-start.16 = (bf16[1,16,16,2304]{3,2,1,0:T(8,128)(2,1)S(1)}, bf16[1,16,16,2304]{3,2,1,0:T(8,128)(2,1)}, u32[]{:S(2)}) copy-start(bf16[1,16,16,2304]{3,2,1,0:T(8,128)(2,1)} %copy-done.15) | copy-start | bytes 3538948
  209.6 9.2 %collective-permute-start.7 = (bf16[1,16,16,256]{3,2,1,0:T(8,128)(2,1)S(1)}, bf16[1,16,16,256]{3,2,1,0:T(8,128)(2,1)S(1)}, u32[]{:S(2)}, u32[]{:S(2)}) collective-permute-start(bf16[1,16,16,256]{3,2,1,0:T(8,128)(2,1)S(1)} %fusion.145), channel_id=1, source_target_pairs={{0,32},{32,64},{64,96},{96,128},{128,160},{160,192},{192,224},{224... | collective-permute-start | bytes 393224 | tf_op jit(solution)/shard_map/ppermute | solution.py:21
  215.3 4.0 copy-start.14
  496.2 5.8 %collective-permute-start.8 = (bf16[72,256]{1,0:T(8,128)(2,1)S(1)}, bf16[72,256]{1,0:T(8,128)(2,1)S(1)}, u32[]{:S(2)}, u32[]{:S(2)}) collective-permute-start(bf16[72,256]{1,0:T(8,128)(2,1)S(1)} %convert_convert_fusion), channel_id=1, source_target_pairs={{0,32},{32,0},{64,96},{96,64},{128,160},{160,128},{192,224},{224,1... | collective-permute-start | bytes 110600 | tf_op jit(solution)/shard_map/ppermute | solution.py:15
  502.0 7.8 %collective-permute-start.9 = (bf16[72,256]{1,0:T(8,128)(2,1)S(1)}, bf16[72,256]{1,0:T(8,128)(2,1)S(1)}, u32[]{:S(2)}, u32[]{:S(2)}) collective-permute-start(bf16[72,256]{1,0:T(8,128)(2,1)S(1)} %collective-permute-done.8), channel_id=1, source_target_pairs={{0,64},{32,96},{64,0},{96,32},{128,192},{160,224},{192,128},{224,1... | collective-permute-start | bytes 110600 | tf_op jit(solution)/shard_map/ppermute | solution.py:15
  509.8 12.6 %copy-start.9 = (bf16[1,16,16,256]{3,2,1,0:T(8,128)(2,1)S(1)}, bf16[1,16,16,256]{3,2,1,0:T(8,128)(2,1)}, u32[]{:S(2)}) copy-start(bf16[1,16,16,256]{3,2,1,0:T(8,128)(2,1)} %copy-done.8) | copy-start | bytes 393220
  509.8 16.2 %copy-start.7 = (f32[1,72,256]{2,1,0:T(8,128)S(1)}, f32[1,72,256]{2,1,0:T(8,128)}, u32[]{:S(2)}) copy-start(f32[1,72,256]{2,1,0:T(8,128)} %param.11) | copy-start | bytes 221188
  509.9 16.2 %copy-start.10 = (f32[1,72,256]{2,1,0:T(8,128)S(1)}, f32[1,72,256]{2,1,0:T(8,128)}, u32[]{:S(2)}) copy-start(f32[1,72,256]{2,1,0:T(8,128)} %param.13) | copy-start | bytes 221188
  509.9 16.2 %copy-start.11 = (f32[1,72,256]{2,1,0:T(8,128)S(1)}, f32[1,72,256]{2,1,0:T(8,128)}, u32[]{:S(2)}) copy-start(f32[1,72,256]{2,1,0:T(8,128)} %param.12) | copy-start | bytes 221188
  509.9 10.3 %collective-permute-start.10 = (bf16[72,256]{1,0:T(8,128)(2,1)S(1)}, bf16[72,256]{1,0:T(8,128)(2,1)S(1)}, u32[]{:S(2)}, u32[]{:S(2)}) collective-permute-start(bf16[72,256]{1,0:T(8,128)(2,1)S(1)} %collective-permute-done.9), channel_id=1, source_target_pairs={{0,128},{32,160},{64,192},{96,224},{128,0},{160,32},{192,64},{224,... | collective-permute-start | bytes 110600 | tf_op jit(solution)/shard_map/ppermute | solution.py:15
  520.2 5.8 %collective-permute-start.11 = (bf16[72,256]{1,0:T(8,128)(2,1)S(1)}, bf16[72,256]{1,0:T(8,128)(2,1)S(1)}, u32[]{:S(2)}, u32[]{:S(2)}) collective-permute-start(bf16[72,256]{1,0:T(8,128)(2,1)S(1)} %collective-permute-done.10), channel_id=1, source_target_pairs={{0,256},{32,288},{64,320},{96,352},{128,384},{160,416},{192,448},{... | collective-permute-start | bytes 110600 | tf_op jit(solution)/shard_map/ppermute | solution.py:15
Sparse Core Ops, SparseCore 0:
  11.8 87.0 all-gather.2
  102.8 80.2 all-gather.4
  221.1 274.2 all-reduce.14
where the time goes:
time: 535 us; the launch traced here: 534 us
  waiting for transfers between devices  360 us (67%)
  local copies, waits for them, and re-layouts  65.3 us (12%)
  starting transfers between devices  57.3 us (11%)
  matrix products  28.5 us (5%)
  between operations  14.5 us (3%)
  other arithmetic  8.8 us (2%)
    psum x1, waiting for transfers between devices, per_device(): lax.psum(term_up.astype(jnp.bfloat16), 'dp').astype(jnp.float32)  257 us
    all_gather x1, waiting for transfers between devices, per_device(): lax.all_gather(mirror_rows, 'dp', axis=0, tiled=True)  51.5 us
    unnamed x126, local copies, waits for them, and re-layouts  40.9 us
    ppermute x8, starting transfers between devices, from_partner(): lax.ppermute(value, axis, [(i, i ^ 1 << stride) for i in range(lax.axis_s...  40 us
    all_gather x1, waiting for transfers between devices, per_device(): lax.all_gather(own_rows, 'dp', axis=0, tiled=True)  35.4 us
    dot_general x6, local copies, waits for them, and re-layouts, section_front(): lax.dot_general(taps_front, kernel, (((1, 2), (0, 2)), ((), ())), preferr...  19.1 us
    ppermute x4, starting transfers between devices, passed_along(): return lax.ppermute(value, axis, pairs)  17.2 us
    dot_general x6, matrix products, section_front(): lax.dot_general(taps_front, kernel, (((1, 2), (0, 2)), ((), ())), preferr...  16.9 us
  transfers between devices with their start and end apart: 15, of which 10 were waited for; matrix products, arithmetic and copies ran while one was open for 15% of the time, Pallas kernels for 0%

commit v1 on v0

--- a/solution.py
+++ b/solution.py
@@ -9,6 +9,11 @@
 learn_rate = 0.01
 decay_rate = 0.1
 epsilon = 1e-08
+
+
+def swapped_in(x, axis, dim):
+    outgoing = jnp.stack([x] * lax.axis_size(axis))
+    return jnp.concatenate(lax.all_to_all(outgoing, axis, 0, 0), axis=dim)
 
 
 def from_partner(value, axis, stride):
@@ -73,7 +78,7 @@
         mirror_rows = from_partner(mirror_rows, "section", bit_number)
     own_weight, mirror_weight = (
         lax.all_gather(own_rows, "dp", axis=0, tiled=True),
-        lax.all_gather(mirror_rows, "dp", axis=0, tiled=True),
+        swapped_in(mirror_rows, "dp", 0),
     )
     grad_down = front_down[0]
     grad_up = front_up[0]

time: 535 us -> 482 us (0.901)
  waiting for transfers between devices: 360 us -> 293 us
  local copies, waits for them, and re-layouts: 65.3 us -> 73.6 us
    all_gather x1 -> x0, waiting for transfers between devices: 51.5 us -> none  [per_device(): lax.all_gather(mirror_rows, 'dp', axis=0, tiled=True)]
    all_gather x1, waiting for transfers between devices: 35.4 us -> 22.5 us  [per_device(): lax.all_gather(own_rows, 'dp', axis=0, tiled=True)]
    all_to_all x0 -> x1, starting transfers between devices: none -> 9.08 us  [swapped_in(): return jnp.concatenate(lax.all_to_all(outgoing, axis, 0, 0), axis=dim)]
    unnamed x126 -> x122, local copies, waits for them, and re-layouts: 40.9 us -> 46 us
  transfers between devices with their start and end apart: 15 -> 15, of which waited for: 10 -> 9; matrix products, arithmetic and copies ran while one was open for 15% -> 19% of each run, Pallas kernels for 0% -> 0%
where the time goes in v1:
time: 482 us; the launch traced here: 481 us
  waiting for transfers between devices  293 us (61%)
  local copies, waits for them, and re-layouts  73.6 us (15%)
  starting transfers between devices  61.9 us (13%)
  matrix products  29 us (6%)
  between operations  14.7 us (3%)
  other arithmetic  8.58 us (2%)
    psum x1, waiting for transfers between devices, per_device(): lax.psum(term_up.astype(jnp.bfloat16), 'dp').astype(jnp.float32)  255 us
    unnamed x122, local copies, waits for them, and re-layouts  46 us
    ppermute x8, starting transfers between devices, from_partner(): lax.ppermute(value, axis, [(i, i ^ 1 << stride) for i in range(lax.axis_s...  40 us
    all_gather x1, waiting for transfers between devices, per_device(): lax.all_gather(own_rows, 'dp', axis=0, tiled=True)  22.5 us
    dot_general x6, local copies, waits for them, and re-layouts, section_front(): lax.dot_general(taps_front, kernel, (((1, 2), (0, 2)), ((), ())), preferr...  19.1 us
    dot_general x6, matrix products, section_front(): lax.dot_general(taps_front, kernel, (((1, 2), (0, 2)), ((), ())), preferr...  16.2 us
    ppermute x4, starting transfers between devices, passed_along(): return lax.ppermute(value, axis, pairs)  12.8 us
    dot_general x6, matrix products, weight_term(): lax.dot_general(taps_hidden, incoming.reshape(-1, channels), (((0,), (0,)...  12.8 us
  transfers between devices with their start and end apart: 15, of which 9 were waited for; matrix products, arithmetic and copies ran while one was open for 19% of the time, Pallas kernels for 0%

profile of v1, /device:TPU:2, one launch (start us, length us, event | category | flops | bytes accessed | tf_op | source)
XLA Modules:
  0.0 481.2 jit_solution(16130331217690836442)
XLA Ops:
  7.2 1.5 bitcast_convert_fusion
  8.8 4.3 collective-permute-start.2
  13.1 1.0 constant_dynamic-update-slice_fusion.8
  14.1 0.9 constant_dynamic-update-slice_fusion.7
  15.0 0.9 constant_dynamic-update-slice_fusion.6
  15.9 0.9 constant_dynamic-update-slice_fusion.5
  26.6 0.9 constant_dynamic-update-slice_fusion.94
  28.7 0.8 pad_slice_fusion.16
  34.3 0.9 constant_dynamic-update-slice_fusion.67
  36.0 0.8 pad_slice_fusion.40
  41.0 6.1 %collective-permute-start.3 = (bf16[72,256]{1,0:T(8,128)(2,1)S(1)}, bf16[72,256]{1,0:T(8,128)(2,1)S(1)}, u32[]{:S(2)}, u32[]{:S(2)}) collective-permute-start(bf16[72,256]{1,0:T(8,128)(2,1)S(1)} %collective-permute-done.2), channel_id=1, source_target_pairs={{0,64},{32,96},{64,0},{96,32},{128,192},{160,224},{192,128},{224,1... | collective-permute-start | bytes 110600 | tf_op jit(solution)/shard_map/ppermute | solution.py:20
  47.8 1.2 collective-permute-done.3
  49.0 9.1 %collective-permute-start.4 = (bf16[72,256]{1,0:T(8,128)(2,1)S(1)}, bf16[72,256]{1,0:T(8,128)(2,1)S(1)}, u32[]{:S(2)}, u32[]{:S(2)}) collective-permute-start(bf16[72,256]{1,0:T(8,128)(2,1)S(1)} %collective-permute-done.3), channel_id=1, source_target_pairs={{0,128},{32,160},{64,192},{96,224},{128,0},{160,32},{192,64},{224,... | collective-permute-start | bytes 110600 | tf_op jit(solution)/shard_map/ppermute | solution.py:20
  58.8 1.3 collective-permute-done.4
  60.1 2.8 collective-permute-start.5
  63.6 3.6 dot_general.48
  67.2 1.1 stack.22
  68.3 9.1 %all-to-all-start = ((bf16[32,72,256]{2,1,0:T(8,128)(2,1)}), bf16[32,72,256]{2,1,0:T(8,128)(2,1)}, u32[]{:S(2)}, u32[]{:S(2)}) async-start(bf16[32,72,256]{2,1,0:T(8,128)(2,1)} %stack.22), calls=%async_computation | async-start | bytes 2359296 | tf_op jit(solution)/shard_map/all_to_all | solution.py:16
  78.1 3.2 fusion.219
  81.4 22.5 %all-gather.2.cloned.1.call-done = bf16[2304,256]{1,0:T(8,128)(2,1)} async-done(((bf16[72,256]{1,0:T(8,128)(2,1)}), bf16[2304,256]{1,0:T(8,128)(2,1)}) %all-gather.2.cloned.1.call-update) | async-done | bytes 1179664 | tf_op jit(solution)/shard_map/all_gather | solution.py:80
  103.9 2.9 fusion.119
  106.8 4.0 collective-permute-start
  111.5 3.6 dot_general.54
  122.0 3.6 dot_general.50
  125.6 2.9 fusion.125
  128.4 4.6 collective-permute-start.1
  133.1 3.0 fusion.139
  136.1 2.1 collective-permute-start.6
  138.3 1.9 convolution_bitcast_fusion.2
  140.2 4.9 %collective-permute-done.6 = bf16[1,16,16,256]{3,2,1,0:T(8,128)(2,1)S(1)} collective-permute-done((bf16[1,16,16,256]{3,2,1,0:T(8,128)(2,1)S(1)}, bf16[1,16,16,256]{3,2,1,0:T(8,128)(2,1)S(1)}, u32[]{:S(2)}, u32[]{:S(2)}) %collective-permute-start.6) | collective-permute-done | bytes 131104 | tf_op jit(solution)/shard_map/ppermute | solution.py:26
  151.4 3.6 dot_general.56
  154.9 3.0 fusion.145
  158.0 2.1 collective-permute-start.7
  160.1 3.7 fusion.7
  163.7 3.4 collective-permute-done.7
  167.6 2.9 fusion.6
  176.9 2.5 dot_general.52
  179.4 2.3 fusion.211
  187.4 254.8 %all-reduce.15.cloned.1.call-done = (bf16[2304,256]{1,0:T(8,128)(2,1)}, bf16[2304,256]{1,0:T(8,128)(2,1)}) async-done(((bf16[2304,256]{1,0:T(8,128)(2,1)}, bf16[2304,256]{1,0:T(8,128)(2,1)}), (bf16[2304,256]{1,0:T(8,128)(2,1)}, bf16[2304,256]{1,0:T(8,128)(2,1)})) %all-reduce.15.cloned.1.call-update) | async-done | bytes 2359312 | tf_op jit(solution)/shard_map/psum | solution.py:107
  443.0 3.5 collective-permute-start.8
  447.2 1.6 collective-permute-done.8
  448.8 4.6 collective-permute-start.9
  454.2 2.4 dot_general.58
  456.7 7.3 %collective-permute-start.10 = (bf16[72,256]{1,0:T(8,128)(2,1)S(1)}, bf16[72,256]{1,0:T(8,128)(2,1)S(1)}, u32[]{:S(2)}, u32[]{:S(2)}) collective-permute-start(bf16[72,256]{1,0:T(8,128)(2,1)S(1)} %collective-permute-done.9), channel_id=1, source_target_pairs={{0,128},{32,160},{64,192},{96,224},{128,0},{160,32},{192,64},{224,... | collective-permute-start | bytes 110600 | tf_op jit(solution)/shard_map/ppermute | solution.py:20
  464.0 2.2 fusion.194
  467.0 2.2 collective-permute-start.11
  470.0 2.8 collective-permute-done.11
  472.8 1.5 convert_bitcast_fusion.8
  (150 shorter events, 53.6 us)
Async XLA Ops:
  7.2 9.7 %copy-start = (bf16[1,1,16,16,256]{4,3,2,1,0:T(8,128)(2,1)S(1)}, bf16[1,1,16,16,256]{4,3,2,1,0:T(8,128)(2,1)}, u32[]{:S(2)}) copy-start(bf16[1,1,16,16,256]{4,3,2,1,0:T(8,128)(2,1)} %param.9) | copy-start | bytes 393220
  7.2 96.7 %all-gather.2.cloned.1.call-start = ((), (), s32[]{:S(2)}) async-start(), calls=%async_computation.1 | async-start | bytes 1216512 | tf_op jit(solution)/shard_map/all_gather | solution.py:80
  8.8 32.2 %collective-permute-start.2 = (bf16[72,256]{1,0:T(8,128)(2,1)}, bf16[72,256]{1,0:T(8,128)(2,1)S(1)}, u32[]{:S(2)}, u32[]{:S(2)}) collective-permute-start(bf16[72,256]{1,0:T(8,128)(2,1)} %bitcast_convert_fusion), channel_id=1, source_target_pairs={{0,32},{32,0},{64,96},{96,64},{128,160},{160,128},{192,224},{224,1... | collective-permute-start | bytes 110600 | tf_op jit(solution)/shard_map/ppermute | solution.py:20
  13.1 4.0 copy-start.1
  17.0 5.6 %copy-start.5 = (bf16[1,16,16,2304]{3,2,1,0:T(8,128)(2,1)}, bf16[1,16,16,2304]{3,2,1,0:T(8,128)(2,1)S(1)}, u32[]{:S(2)}) copy-start(bf16[1,16,16,2304]{3,2,1,0:T(8,128)(2,1)S(1)} %constant_dynamic-update-slice_fusion) | copy-start | bytes 3538948
  17.1 6.3 %copy-start.4 = (bf16[3,1,1,16,16,256]{5,4,3,2,1,0:T(8,128)(2,1)S(1)}, bf16[3,1,1,16,16,256]{5,4,3,2,1,0:T(8,128)(2,1)}, u32[]{:S(2)}) copy-start(bf16[3,1,1,16,16,256]{5,4,3,2,1,0:T(8,128)(2,1)} %param.8) | copy-start | bytes 1179652
  27.7 1.1 copy-start.13
  29.6 1.6 copy-start.3
  41.0 17.9 %copy-start.15 = (bf16[1,16,16,2304]{3,2,1,0:T(8,128)(2,1)}, bf16[1,16,16,2304]{3,2,1,0:T(8,128)(2,1)S(1)}, u32[]{:S(2)}) copy-start(bf16[1,16,16,2304]{3,2,1,0:T(8,128)(2,1)S(1)} %constant_dynamic-update-slice_fusion.72) | copy-start | bytes 3538948
  41.0 8.0 %collective-permute-start.3 = (bf16[72,256]{1,0:T(8,128)(2,1)S(1)}, bf16[72,256]{1,0:T(8,128)(2,1)S(1)}, u32[]{:S(2)}, u32[]{:S(2)}) collective-permute-start(bf16[72,256]{1,0:T(8,128)(2,1)S(1)} %collective-permute-done.2), channel_id=1, source_target_pairs={{0,64},{32,96},{64,0},{96,32},{128,192},{160,224},{192,128},{224,1... | collective-permute-start | bytes 110600 | tf_op jit(solution)/shard_map/ppermute | solution.py:20
  49.0 11.1 %collective-permute-start.4 = (bf16[72,256]{1,0:T(8,128)(2,1)S(1)}, bf16[72,256]{1,0:T(8,128)(2,1)S(1)}, u32[]{:S(2)}, u32[]{:S(2)}) collective-permute-start(bf16[72,256]{1,0:T(8,128)(2,1)S(1)} %collective-permute-done.3), channel_id=1, source_target_pairs={{0,128},{32,160},{64,192},{96,224},{128,0},{160,32},{192,64},{224,... | collective-permute-start | bytes 110600 | tf_op jit(solution)/shard_map/ppermute | solution.py:20
  60.1 7.1 %collective-permute-start.5 = (bf16[72,256]{1,0:T(8,128)(2,1)S(1)}, bf16[72,256]{1,0:T(8,128)(2,1)S(1)}, u32[]{:S(2)}, u32[]{:S(2)}) collective-permute-start(bf16[72,256]{1,0:T(8,128)(2,1)S(1)} %collective-permute-done.4), channel_id=1, source_target_pairs={{0,256},{32,288},{64,320},{96,352},{128,384},{160,416},{192,448},{... | collective-permute-start | bytes 110600 | tf_op jit(solution)/shard_map/ppermute | solution.py:20
  68.3 64.8 %all-to-all-start = ((bf16[32,72,256]{2,1,0:T(8,128)(2,1)}), bf16[32,72,256]{2,1,0:T(8,128)(2,1)}, u32[]{:S(2)}, u32[]{:S(2)}) async-start(bf16[32,72,256]{2,1,0:T(8,128)(2,1)} %stack.22), calls=%async_computation | async-start | bytes 2359296 | tf_op jit(solution)/shard_map/all_to_all | solution.py:16
  77.4 364.8 %all-reduce.15.cloned.1.call-start = ((), (), s32[]{:S(2)}) async-start(), calls=%async_computation.2 | async-start | bytes 4718592 | tf_op jit(solution)/shard_map/psum | solution.py:107
  106.8 9.0 %collective-permute-start = (bf16[1,16,16,256]{3,2,1,0:T(8,128)(2,1)S(1)}, bf16[1,16,16,256]{3,2,1,0:T(8,128)(2,1)S(1)}, u32[]{:S(2)}, u32[]{:S(2)}) collective-permute-start(bf16[1,16,16,256]{3,2,1,0:T(8,128)(2,1)S(1)} %bitcast.548), channel_id=1, source_target_pairs={{32,0},{64,32},{96,64},{128,96},{160,128},{192,160},{224,192},{256... | collective-permute-start | bytes 393224 | tf_op jit(solution)/shard_map/ppermute | solution.py:26
  128.4 7.7 %copy-start.9 = (bf16[1,16,16,256]{3,2,1,0:T(8,128)(2,1)}, bf16[1,16,16,256]{3,2,1,0:T(8,128)(2,1)S(1)}, u32[]{:S(2)}) copy-start(bf16[1,16,16,256]{3,2,1,0:T(8,128)(2,1)S(1)} %fusion.125) | copy-start | bytes 393220
  128.4 9.8 %collective-permute-start.1 = (bf16[1,16,16,256]{3,2,1,0:T(8,128)(2,1)S(1)}, bf16[1,16,16,256]{3,2,1,0:T(8,128)(2,1)S(1)}, u32[]{:S(2)}, u32[]{:S(2)}) collective-permute-start(bf16[1,16,16,256]{3,2,1,0:T(8,128)(2,1)S(1)} %fusion.125), channel_id=1, source_target_pairs={{32,0},{64,32},{96,64},{128,96},{160,128},{192,160},{224,192},{256... | collective-permute-start | bytes 393224 | tf_op jit(solution)/shard_map/ppermute | solution.py:26
  133.1 5.1 %copy-start.16 = (bf16[1,16,16,2304]{3,2,1,0:T(8,128)(2,1)S(1)}, bf16[1,16,16,2304]{3,2,1,0:T(8,128)(2,1)}, u32[]{:S(2)}) copy-start(bf16[1,16,16,2304]{3,2,1,0:T(8,128)(2,1)} %copy-done.15) | copy-start | bytes 3538948
  136.1 9.0 %collective-permute-start.6 = (bf16[1,16,16,256]{3,2,1,0:T(8,128)(2,1)S(1)}, bf16[1,16,16,256]{3,2,1,0:T(8,128)(2,1)S(1)}, u32[]{:S(2)}, u32[]{:S(2)}) collective-permute-start(bf16[1,16,16,256]{3,2,1,0:T(8,128)(2,1)S(1)} %bitcast.546), channel_id=1, source_target_pairs={{0,32},{32,64},{64,96},{96,128},{128,160},{160,192},{192,224},{224... | collective-permute-start | bytes 393224 | tf_op jit(solution)/shard_map/ppermute | solution.py:26
  154.9 5.1 %copy-start.2 = (f32[2304,256]{1,0:T(8,128)S(1)}, f32[2304,256]{1,0:T(8,128)}, u32[]{:S(2)}) copy-start(f32[2304,256]{1,0:T(8,128)} %fusion.219) | copy-start | bytes 7077892
  158.0 5.8 %copy-start.7 = (bf16[1,16,16,256]{3,2,1,0:T(8,128)(2,1)}, bf16[1,16,16,256]{3,2,1,0:T(8,128)(2,1)S(1)}, u32[]{:S(2)}) copy-start(bf16[1,16,16,256]{3,2,1,0:T(8,128)(2,1)S(1)} %fusion.145) | copy-start | bytes 393220
  158.0 9.1 %copy-start.14 = (bf16[1,16,16,2304]{3,2,1,0:T(8,128)(2,1)S(1)}, bf16[1,16,16,2304]{3,2,1,0:T(8,128)(2,1)}, u32[]{:S(2)}) copy-start(bf16[1,16,16,2304]{3,2,1,0:T(8,128)(2,1)} %copy-done.13) | copy-start | bytes 3538948
  158.0 9.1 %collective-permute-start.7 = (bf16[1,16,16,256]{3,2,1,0:T(8,128)(2,1)S(1)}, bf16[1,16,16,256]{3,2,1,0:T(8,128)(2,1)S(1)}, u32[]{:S(2)}, u32[]{:S(2)}) collective-permute-start(bf16[1,16,16,256]{3,2,1,0:T(8,128)(2,1)S(1)} %fusion.145), channel_id=1, source_target_pairs={{0,32},{32,64},{64,96},{96,128},{128,160},{160,192},{192,224},{224... | collective-permute-start | bytes 393224 | tf_op jit(solution)/shard_map/ppermute | solution.py:26
  179.4 2.3 copy-start.10
  443.0 5.8 %collective-permute-start.8 = (bf16[72,256]{1,0:T(8,128)(2,1)S(1)}, bf16[72,256]{1,0:T(8,128)(2,1)S(1)}, u32[]{:S(2)}, u32[]{:S(2)}) collective-permute-start(bf16[72,256]{1,0:T(8,128)(2,1)S(1)} %convert_convert_fusion), channel_id=1, source_target_pairs={{0,32},{32,0},{64,96},{96,64},{128,160},{160,128},{192,224},{224,1... | collective-permute-start | bytes 110600 | tf_op jit(solution)/shard_map/ppermute | solution.py:20
  448.8 7.8 %collective-permute-start.9 = (bf16[72,256]{1,0:T(8,128)(2,1)S(1)}, bf16[72,256]{1,0:T(8,128)(2,1)S(1)}, u32[]{:S(2)}, u32[]{:S(2)}) collective-permute-start(bf16[72,256]{1,0:T(8,128)(2,1)S(1)} %collective-permute-done.8), channel_id=1, source_target_pairs={{0,64},{32,96},{64,0},{96,32},{128,192},{160,224},{192,128},{224,1... | collective-permute-start | bytes 110600 | tf_op jit(solution)/shard_map/ppermute | solution.py:20
  456.6 12.6 %copy-start.8 = (bf16[1,16,16,256]{3,2,1,0:T(8,128)(2,1)S(1)}, bf16[1,16,16,256]{3,2,1,0:T(8,128)(2,1)}, u32[]{:S(2)}) copy-start(bf16[1,16,16,256]{3,2,1,0:T(8,128)(2,1)} %copy-done.7) | copy-start | bytes 393220
  456.6 16.2 %copy-start.6 = (f32[1,72,256]{2,1,0:T(8,128)S(1)}, f32[1,72,256]{2,1,0:T(8,128)}, u32[]{:S(2)}) copy-start(f32[1,72,256]{2,1,0:T(8,128)} %param.11) | copy-start | bytes 221188
  456.7 16.2 %copy-start.11 = (f32[1,72,256]{2,1,0:T(8,128)S(1)}, f32[1,72,256]{2,1,0:T(8,128)}, u32[]{:S(2)}) copy-start(f32[1,72,256]{2,1,0:T(8,128)} %param.13) | copy-start | bytes 221188
  456.7 16.2 %copy-start.12 = (f32[1,72,256]{2,1,0:T(8,128)S(1)}, f32[1,72,256]{2,1,0:T(8,128)}, u32[]{:S(2)}) copy-start(f32[1,72,256]{2,1,0:T(8,128)} %param.12) | copy-start | bytes 221188
  456.7 10.3 %collective-permute-start.10 = (bf16[72,256]{1,0:T(8,128)(2,1)S(1)}, bf16[72,256]{1,0:T(8,128)(2,1)S(1)}, u32[]{:S(2)}, u32[]{:S(2)}) collective-permute-start(bf16[72,256]{1,0:T(8,128)(2,1)S(1)} %collective-permute-done.9), channel_id=1, source_target_pairs={{0,128},{32,160},{64,192},{96,224},{128,0},{160,32},{192,64},{224,... | collective-permute-start | bytes 110600 | tf_op jit(solution)/shard_map/ppermute | solution.py:20
  467.0 5.8 %collective-permute-start.11 = (bf16[72,256]{1,0:T(8,128)(2,1)S(1)}, bf16[72,256]{1,0:T(8,128)(2,1)S(1)}, u32[]{:S(2)}, u32[]{:S(2)}) collective-permute-start(bf16[72,256]{1,0:T(8,128)(2,1)S(1)} %collective-permute-done.10), channel_id=1, source_target_pairs={{0,256},{32,288},{64,320},{96,352},{128,384},{160,416},{192,448},{... | collective-permute-start | bytes 110600 | tf_op jit(solution)/shard_map/ppermute | solution.py:20
Sparse Core Ops, SparseCore 0:
  11.8 92.0 all-gather.1
  170.7 271.4 all-reduce.14
